TPU v7x, 32 devices: a whole 2x2x4 slice. The times are simulated.
32 devices in a mesh: dom: 8 (over z, x), band: 4 (over y, core).
Axes of the slice: x: 2, y: 2, z: 4, core: 2. Of those that a mesh axis runs over, the one named last changes fastest.
Arguments:
- orbitals: float32 [32, 96, 64, 128], P('band', 'dom'), may hold values from -1400 to 1400
- potential: float32 [96, 64, 128], P('dom'), may hold values from 0.1 to 2
Outputs:
- ortho_orbitals: float32 [32, 96, 64, 128], P('band', 'dom')
All inputs are finite; a program needn't handle non-finite values.
Results may differ from a plain program's by a relative error of at most 0.0003.
Values sent between devices are 32-bit elements; how exact they have to be, the bound alone decides.
A program may use at most 64 MiB of HBM per device.

v0:
```python
import jax
import jax.numpy as jnp
from jax import lax
from jax.sharding import PartitionSpec as P

stencil_weights = [
    -5369.0 / 1800.0,
    12.0 / 7.0,
    -15.0 / 56.0,
    10.0 / 189.0,
    -1.0 / 112.0,
    2.0 / 1925.0,
    -1.0 / 16632.0,
]
center_shift = 9.5
half_width = 7.5


def padded_2(block, sides, width):
    for axis, dim in sides:
        count = lax.axis_size(axis)
        forward = [(i, i + 1) for i in range(count - 1)]
        backward = [(target, source) for source, target in forward]
        low = lax.ppermute(
            lax.slice_in_dim(block, block.shape[dim] - width, None, axis=dim), axis, forward
        )
        high = lax.ppermute(lax.slice_in_dim(block, 0, width, axis=dim), axis, backward)
        block = jnp.concatenate([low, block, high], axis=dim)
    return block


def apply_hamiltonian(padded, field_potential):
    length = field_potential.shape[0]
    inner = padded[:, 6 : 6 + length]
    rows_y = inner.shape[2]
    rows_z = inner.shape[3]
    spread = jnp.pad(inner, ((0, 0), (0, 0), (6, 6), (6, 6)))
    laplace = 3.0 * stencil_weights[0] * inner
    for offset in range(1, 7):
        near = (
            padded[:, 6 + offset : 6 + offset + length]
            + padded[:, 6 - offset : 6 - offset + length]
        )
        near = (
            near
            + spread[:, :, 6 + offset : 6 + offset + rows_y, 6 : 6 + rows_z]
            + spread[:, :, 6 - offset : 6 - offset + rows_y, 6 : 6 + rows_z]
        )
        near = (
            near
            + spread[:, :, 6 : 6 + rows_y, 6 + offset : 6 + offset + rows_z]
            + spread[:, :, 6 : 6 + rows_y, 6 - offset : 6 - offset + rows_z]
        )
        laplace = laplace + stencil_weights[offset] * near
    return -0.5 * laplace + field_potential * inner


def shards(orbitals, potential):
    own_rows = orbitals.shape[1]
    padded = padded_2(orbitals, (("dom", 1),), 6)
    first = (apply_hamiltonian(padded, potential) - center_shift * orbitals) / half_width
    padded_first = padded_2(first, (("dom", 1),), 6)
    filtered = (
        2.0 * (apply_hamiltonian(padded_first, potential) - center_shift * first) / half_width
        - orbitals
    )
    cells = lax.all_to_all(filtered, "band", split_axis=2, concat_axis=0, tiled=True)
    count = cells.shape[0]
    flat = cells.reshape(count, -1)
    partial_correlation = jnp.dot(
        flat, flat.T, precision=lax.Precision.HIGHEST, preferred_element_type=jnp.float32
    )
    all_cells = own_rows * lax.axis_size("dom") * orbitals.shape[2] * orbitals.shape[3]
    correlation = lax.psum(partial_correlation, ("dom", "band")) / jnp.float32(all_cells)
    lower = jnp.linalg.cholesky(correlation)
    inverse = lax.linalg.triangular_solve(
        lower, jnp.eye(count, dtype=correlation.dtype), left_side=True, lower=True
    )
    ortho = jnp.dot(
        inverse, flat, precision=lax.Precision.HIGHEST, preferred_element_type=jnp.float32
    ).reshape(cells.shape)
    return lax.all_to_all(ortho, "band", split_axis=0, concat_axis=2, tiled=True)


def solution(mesh):
    in_specs = (P("band", "dom", None, None), P("dom", None, None))
    out_specs = P("band", "dom", None, None)
    return jax.shard_map(shards, mesh=mesh, in_specs=in_specs, out_specs=out_specs, check_vma=False)
```

profile of v0, /device:TPU:5, one launch (start us, length us, event | category | flops | bytes accessed | tf_op | source)
XLA Modules:
  0.0 319.6 jit_solution(681666642300067285)
XLA Ops:
  0.0 2.2 fusion.103
  2.2 3.5 %collective-permute-start.1 = (f32[8,6,64,128]{3,2,1,0:T(8,128)S(1)}, f32[8,6,64,128]{3,2,1,0:T(8,128)S(1)}, u32[]{:S(2)}, u32[]{:S(2)}) collective-permute-start(f32[8,6,64,128]{3,2,1,0:T(8,128)S(1)} %get-tuple-element.10), channel_id=1, source_target_pairs={{0,4},{4,8},{8,12},{12,16},{16,20},{20,24},{24,28},{1,5},{5,9},{9,... | collective-permute-start | bytes 4718600 | tf_op jit(solution)/shard_map/ppermute | solution.py:24
  5.7 1.3 collective-permute-start
  7.0 65.4 %collective-permute-done.1 = f32[8,6,64,128]{3,2,1,0:T(8,128)S(1)} collective-permute-done((f32[8,6,64,128]{3,2,1,0:T(8,128)S(1)}, f32[8,6,64,128]{3,2,1,0:T(8,128)S(1)}, u32[]{:S(2)}, u32[]{:S(2)}) %collective-permute-start.1) | collective-permute-done | bytes 1572896 | tf_op jit(solution)/shard_map/ppermute | solution.py:24
  72.4 0.1 constant_dynamic-update-slice_fusion.3
  72.5 0.9 constant_dynamic-update-slice_fusion.1
  73.4 0.2 constant_dynamic-update-slice_fusion
  73.6 0.8 copy-done.3
  74.4 11.5 %broadcast_multiply_fusion = (f32[8,12,64,128]{3,2,1,0:T(8,128)}, f32[8,12,64,128]{3,2,1,0:T(8,128)}) fusion(f32[8,12,64,128]{3,2,1,0:T(8,128)S(1)} %copy-done, f32[12,64,128]{2,1,0:T(8,128)S(1)} %copy-done.3, f32[8,18,64,128]{3,2,1,0:T(8,128)S(1)} %get-tuple-element.12, f32[8,18,64,128]{3,2,1,0:T(8,128)S(1)} %constant_dynamic-update-slice_fusion), kind=kLoop, calls=%fused_computation.175 | loop fusion | flops 38535168 | bytes 47579136 | tf_op jit(solution)/shard_map/div | solution.py:61
  85.9 2.3 fusion.102
  88.2 1.4 collective-permute-start.2
  89.6 4.8 %collective-permute-start.3 = (f32[8,6,64,128]{3,2,1,0:T(8,128)S(1)}, f32[8,6,64,128]{3,2,1,0:T(8,128)S(1)}, u32[]{:S(2)}, u32[]{:S(2)}) collective-permute-start(f32[8,6,64,128]{3,2,1,0:T(8,128)S(1)} %get-tuple-element.8), channel_id=1, source_target_pairs={{0,4},{4,8},{8,12},{12,16},{16,20},{20,24},{24,28},{1,5},{5,9},{9,... | collective-permute-start | bytes 4718600 | tf_op jit(solution)/shard_map/ppermute | solution.py:24
  94.5 31.2 %collective-permute-done.2 = f32[8,6,64,128]{3,2,1,0:T(8,128)S(1)} collective-permute-done((f32[8,6,64,128]{3,2,1,0:T(8,128)S(1)}, f32[8,6,64,128]{3,2,1,0:T(8,128)S(1)}, u32[]{:S(2)}, u32[]{:S(2)}) %collective-permute-start.2) | collective-permute-done | bytes 1572896 | tf_op jit(solution)/shard_map/ppermute | solution.py:27
  125.6 35.5 %collective-permute-done.3 = f32[8,6,64,128]{3,2,1,0:T(8,128)S(1)} collective-permute-done((f32[8,6,64,128]{3,2,1,0:T(8,128)S(1)}, f32[8,6,64,128]{3,2,1,0:T(8,128)S(1)}, u32[]{:S(2)}, u32[]{:S(2)}) %collective-permute-start.3) | collective-permute-done | bytes 1572896 | tf_op jit(solution)/shard_map/ppermute | solution.py:24
  161.1 1.1 copy-done.4
  162.3 11.9 %fusion.13 = f32[8,12,64,128]{3,2,1,0:T(8,128)S(1)} fusion(f32[8,12,64,128]{3,2,1,0:T(8,128)S(1)} %copy-done, f32[8,12,64,128]{3,2,1,0:T(8,128)S(1)} %copy-done.1, f32[8,6,64,128]{3,2,1,0:T(8,128)} %copy-done.4, f32[8,6,64,128]{3,2,1,0:T(8,128)S(1)} %collective-permute-done.2, f32[8,12,64,128]{3,2,1,0:T(8,128)S(1)} %copy-done.2, ...), kind=kLoop, calls=%fused_computation.81 | loop fusion | flops 48758784 | bytes 16121856 | tf_op jit(solution)/shard_map/sub | solution.py:64
  174.2 1.8 copy.28
  176.0 38.1 %all_to_all.33 = f32[8,12,64,128]{3,0,1,2:T(8,128)S(1)} all-to-all(f32[8,12,64,128]{3,0,1,2:T(8,128)S(1)} %copy.28), channel_id=1, replica_groups=mesh['dom'=8,'band'=4] {'band'}, dimensions={2} | all-to-all | bytes 6291456 | tf_op jit(solution)/shard_map/all_to_all | solution.py:67
  214.2 3.5 %copy.41 = f32[8,12,4,16,128]{4,3,1,0,2:T(8,128)} copy(f32[8,12,4,16,128]{4,0,1,3,2:T(8,128)S(1)} %bitcast.34) | data formatting | bytes 6291456 | tf_op jit(solution)/shard_map/all_to_all | solution.py:67
  217.7 2.2 reshape.16
  219.9 2.6 fusion.104
  222.4 41.9 %psum.7 = f32[32,32]{0,1:T(8,128)S(1)} all-reduce(f32[32,32]{0,1:T(8,128)S(1)} %fusion.104), channel_id=1, replica_groups=mesh['dom'=8,'band'=4] {'dom','band'}, use_global_device_ids=true, to_apply=%region_0.1 | all-reduce | flops 1024 | bytes 8192 | tf_op jit(solution)/shard_map/psum | solution.py:74
  264.4 2.9 cholesky.17
  267.4 0.6 compare_reduce_fusion
  268.0 0.7 fusion.98
  268.7 2.4 custom-call.6
  271.1 0.2 convolution_bitcast_fusion
  271.3 0.6 copy.37
  271.9 4.6 %fusion.96 = f32[32,12,16,128]{3,0,2,1:T(8,128)S(1)} fusion(f32[32,32,1,1]{1,0,3,2:T(8,128)S(1)} %convolution_bitcast_fusion, f32[12,16,128,32]{2,1,0,3:T(8,128)S(1)} %bitcast.33), kind=kOutput, calls=%fused_computation.172 | convolution fusion | flops 301989888 | bytes 6295552 | tf_op jit(solution)/shard_map/dot_general | solution.py:79
  276.5 1.8 copy.33
  278.3 39.1 %all_to_all.34 = f32[32,12,16,128]{3,2,1,0:T(8,128)S(1)} all-to-all(f32[32,12,16,128]{3,2,1,0:T(8,128)S(1)} %copy.33), channel_id=1, replica_groups=mesh['dom'=8,'band'=4] {'band'}, dimensions={0} | all-to-all | bytes 6291456 | tf_op jit(solution)/shard_map/all_to_all | solution.py:82
  317.5 2.1 copy.34
  (14 shorter events, 0.2 us)
Async XLA Ops:
  2.2 70.3 %copy-start = (f32[8,12,64,128]{3,2,1,0:T(8,128)S(1)}, f32[8,12,64,128]{3,2,1,0:T(8,128)}, u32[]{:S(2)}) copy-start(f32[8,12,64,128]{3,2,1,0:T(8,128)} %param.2) | copy-start | bytes 9437188
  2.2 70.2 %collective-permute-start.1 = (f32[8,6,64,128]{3,2,1,0:T(8,128)S(1)}, f32[8,6,64,128]{3,2,1,0:T(8,128)S(1)}, u32[]{:S(2)}, u32[]{:S(2)}) collective-permute-start(f32[8,6,64,128]{3,2,1,0:T(8,128)S(1)} %get-tuple-element.10), channel_id=1, source_target_pairs={{0,4},{4,8},{8,12},{12,16},{16,20},{20,24},{24,28},{1,5},{5,9},{9,... | collective-permute-start | bytes 4718600 | tf_op jit(solution)/shard_map/ppermute | solution.py:24
  5.7 67.7 %collective-permute-start = (f32[8,6,64,128]{3,2,1,0:T(8,128)S(1)}, f32[8,6,64,128]{3,2,1,0:T(8,128)S(1)}, u32[]{:S(2)}, u32[]{:S(2)}) collective-permute-start(f32[8,6,64,128]{3,2,1,0:T(8,128)S(1)} %get-tuple-element.9), channel_id=1, source_target_pairs={{4,0},{8,4},{12,8},{16,12},{20,16},{24,20},{28,24},{5,1},{9,5},{13... | collective-permute-start | bytes 4718600 | tf_op jit(solution)/shard_map/ppermute | solution.py:27
  73.4 1.0 copy-start.3
  85.9 76.4 %copy-start.1 = (f32[8,12,64,128]{3,2,1,0:T(8,128)S(1)}, f32[8,12,64,128]{3,2,1,0:T(8,128)}, u32[]{:S(2)}) copy-start(f32[8,12,64,128]{3,2,1,0:T(8,128)} %get-tuple-element.5) | copy-start | bytes 9437188
  85.9 76.4 %copy-start.2 = (f32[8,12,64,128]{3,2,1,0:T(8,128)S(1)}, f32[8,12,64,128]{3,2,1,0:T(8,128)}, u32[]{:S(2)}) copy-start(f32[8,12,64,128]{3,2,1,0:T(8,128)} %get-tuple-element.6) | copy-start | bytes 9437188
  88.2 37.5 %collective-permute-start.2 = (f32[8,6,64,128]{3,2,1,0:T(8,128)S(1)}, f32[8,6,64,128]{3,2,1,0:T(8,128)S(1)}, u32[]{:S(2)}, u32[]{:S(2)}) collective-permute-start(f32[8,6,64,128]{3,2,1,0:T(8,128)S(1)} %get-tuple-element.7), channel_id=1, source_target_pairs={{4,0},{8,4},{12,8},{16,12},{20,16},{24,20},{28,24},{5,1},{9,5},{13... | collective-permute-start | bytes 4718600 | tf_op jit(solution)/shard_map/ppermute | solution.py:27
  89.6 71.5 %collective-permute-start.3 = (f32[8,6,64,128]{3,2,1,0:T(8,128)S(1)}, f32[8,6,64,128]{3,2,1,0:T(8,128)S(1)}, u32[]{:S(2)}, u32[]{:S(2)}) collective-permute-start(f32[8,6,64,128]{3,2,1,0:T(8,128)S(1)} %get-tuple-element.8), channel_id=1, source_target_pairs={{0,4},{4,8},{8,12},{12,16},{16,20},{20,24},{24,28},{1,5},{5,9},{9,... | collective-permute-start | bytes 4718600 | tf_op jit(solution)/shard_map/ppermute | solution.py:24
  161.1 1.1 copy-start.4
where the time goes:
time: 323 us; the launch traced here: 320 us
  waiting for transfers between devices  132 us (41%)
  blocking collectives  119 us (37%)
  other arithmetic  30.1 us (9%)
  local copies, waits for them, and re-layouts  19.7 us (6%)
  starting transfers between devices  11 us (3%)
  matrix products  7.36 us (2%)
    ppermute x2, waiting for transfers between devices, padded_2(): lax.ppermute(lax.slice_in_dim(block, block.shape[dim] - width, None, axis...  101 us
    psum x1, blocking collectives, shards(): lax.psum(partial_correlation, ('dom', 'band')) / jnp.float32(all_cells)  41.9 us
    all_to_all x1, blocking collectives, shards(): lax.all_to_all(ortho, 'band', split_axis=0, concat_axis=2, tiled=True)  39.1 us
    all_to_all x1, blocking collectives, shards(): lax.all_to_all(filtered, 'band', split_axis=2, concat_axis=0, tiled=True)  38.1 us
    ppermute x2, waiting for transfers between devices, padded_2(): lax.ppermute(lax.slice_in_dim(block, 0, width, axis=dim), axis, backward)  31.2 us
    sub x1, other arithmetic, shards(): 2.0 * (apply_hamiltonian(padded_first, potential) - center_shift * first)  11.9 us
    div x1, other arithmetic, shards(): (apply_hamiltonian(padded, potential) - center_shift * orbitals) / half_w...  11.5 us
    ppermute x2, starting transfers between devices, padded_2(): lax.ppermute(lax.slice_in_dim(block, block.shape[dim] - width, None, axis...  8.31 us
  transfers between devices with their start and end apart: 4, of which 3 were waited for; matrix products, arithmetic and copies ran while one was open for 0% of the time, Pallas kernels for 0%

commit v1 on v0

v1 whole, which is shorter than its diff:
```python
import functools
import jax
import jax.numpy as jnp
from jax import lax
from jax.experimental import pallas as pl
from jax.experimental.pallas import tpu as pltpu
from jax.sharding import PartitionSpec as P

stencil_weights = [
    -5369.0 / 1800.0,
    12.0 / 7.0,
    -15.0 / 56.0,
    10.0 / 189.0,
    -1.0 / 112.0,
    2.0 / 1925.0,
    -1.0 / 16632.0,
]
center_shift = 9.5
half_width = 7.5
reach = 6
pad = 8
scaled = [-0.5 * w / half_width for w in stencil_weights]
HIGHEST = lax.Precision.HIGHEST


def divisor(n, options):
    for c in options:
        if n % c == 0:
            return c
    return 1


def kernel(
    doms, bands, nb, nx, ny, nz,
    orb, pot, bz, out,
    u, f, filt, potb, cells, obuf, gs, ar1, ar2, inv,
    own_sem, pot_sem, swap_s, swap_r, h1_s, h1_r, h2_s, h2_r,
    a2a_s, a2a_r, a2a_l, r1_s, r1_r, r2_s, r2_r, ret_s, ret_r, ret_l,
):
    half = nb // 2
    planes = 2 * nx
    total = nb * bands
    group = 2 * bands
    slab = nx * ny
    share = slab // bands
    dom = lax.axis_index("dom")
    band = lax.axis_index("band")
    layer = dom // 2
    layers = doms // 2
    side = dom % 2
    base = layer * 2
    me = side * bands + band
    partner = {"dom": base + 1 - side, "band": band}

    def peer(j):
        g = (me + j) % group
        return g // bands, g % bands

    def peer_id(j):
        q, b = peer(j)
        return {"dom": base + q, "band": b}

    def layer_id(j):
        return {"dom": ((layer + j) % layers) * 2 + side, "band": band}

    barrier = pltpu.get_barrier_semaphore()
    for j in range(1, group):
        pl.semaphore_signal(barrier, inc=1, device_id=peer_id(j), device_id_type=pl.DeviceIdType.MESH)
    for j in range(1, layers):
        pl.semaphore_signal(barrier, inc=1, device_id=layer_id(j), device_id_type=pl.DeviceIdType.MESH)
    pl.semaphore_wait(barrier, group - 1 + layers - 1)

    def remote(src, dst, s, r, dev):
        return pltpu.make_async_remote_copy(
            src_ref=src, dst_ref=dst, send_sem=s, recv_sem=r,
            device_id=dev, device_id_type=pl.DeviceIdType.MESH,
        )

    rows = pl.ds(pad, ny)
    mine = pl.ds(reach + side * nx, nx)

    def swap(o):
        return remote(
            orb.at[(1 - side) * half + o], u.at[o, mine, rows], swap_s.at[o], swap_r.at[o], partner
        )

    swap_pot = remote(pot, potb.at[pl.ds(side * nx, nx)], swap_s.at[half], swap_r.at[half], partner)

    def own(o):
        return pltpu.make_async_copy(orb.at[side * half + o], u.at[o, mine, rows], own_sem.at[o])

    own_pot = pltpu.make_async_copy(pot, potb.at[pl.ds(side * nx, nx)], pot_sem)

    swap(0).start()
    swap_pot.start()
    for o in range(1, half):
        swap(o).start()
    for o in range(half):
        own(o).start()
    own_pot.start()

    def up(buf, o, s, r):
        return remote(
            buf.at[o, pl.ds(planes, reach), rows], buf.at[o, pl.ds(0, reach), rows],
            s.at[0, o], r.at[0, o], {"dom": dom + 2, "band": band},
        )

    def down(buf, o, s, r):
        return remote(
            buf.at[o, pl.ds(reach, reach), rows], buf.at[o, pl.ds(planes + reach, reach), rows],
            s.at[1, o], r.at[1, o], {"dom": dom - 2, "band": band},
        )

    has_up = layer < layers - 1
    has_down = layer > 0

    def send_halos(buf, o, s, r):
        @pl.when(has_up)
        def _():
            up(buf, o, s, r).start()

        @pl.when(has_down)
        def _():
            down(buf, o, s, r).start()

    def wait_halos(buf, o, s, r):
        @pl.when(has_down)
        def _():
            up(buf, o, s, r).wait_recv()

        @pl.when(has_up)
        def _():
            down(buf, o, s, r).wait_recv()

    edge = jnp.zeros((planes + 2 * reach, pad, nz), jnp.float32)
    for buf in (u, f):
        for o in range(half):
            buf[o, :, pl.ds(0, pad), :] = edge
            buf[o, :, pl.ds(pad + ny, pad), :] = edge
    empty = jnp.zeros((reach, ny, nz), jnp.float32)
    for buf in (u, f):
        for o in range(half):
            @pl.when(jnp.logical_not(has_down))
            def _():
                buf[o, pl.ds(0, reach), rows, :] = empty

            @pl.when(jnp.logical_not(has_up))
            def _():
                buf[o, pl.ds(planes + reach, reach), rows, :] = empty

    step = divisor(planes, (4, 3, 2))

    def apply(buf, o, emit):
        def body(t, carry):
            x0 = t * step
            centre = [buf[o, reach + x0 + i, pl.ds(pad, ny), :] for i in range(step)]
            along_z = jnp.dot(
                jnp.concatenate(centre, axis=0), bz[...], precision=HIGHEST,
                preferred_element_type=jnp.float32,
            )
            for i in range(step):
                x = reach + x0 + i
                weight = potb[x0 + i] * (1.0 / half_width) + (
                    3.0 * scaled[0] - center_shift / half_width
                )
                acc = along_z[i * ny:(i + 1) * ny] + weight * centre[i]
                for k in range(1, reach + 1):
                    near = buf[o, x + k, pl.ds(pad, ny), :] + buf[o, x - k, pl.ds(pad, ny), :]
                    near = near + (
                        buf[o, x, pl.ds(pad + k, ny), :] + buf[o, x, pl.ds(pad - k, ny), :]
                    )
                    acc = acc + scaled[k] * near
                emit(x0 + i, acc)
            return carry

        lax.fori_loop(0, planes // step, body, 0)

    def stage_a(o):
        own(o).wait()
        swap(o).wait_recv()
        send_halos(u, o, h1_s, h1_r)

    def stage_b(o):
        wait_halos(u, o, h1_s, h1_r)

        def emit(x, acc):
            f[o, reach + x, pl.ds(pad, ny), :] = acc

        apply(u, o, emit)
        send_halos(f, o, h2_s, h2_r)

    def a2a(o, j):
        q, b = peer(j)
        first = pl.multiple_of(q * slab + b * share, 8)
        to = pl.multiple_of((band * nb + side * half + o) * share, 8)
        return remote(
            filt.at[o, pl.ds(first, share)], cells.at[pl.ds(to, share)],
            a2a_s.at[j - 1, o], a2a_r.at[j - 1, o], peer_id(j),
        )

    def a2a_own(o):
        first = pl.multiple_of(me * share, 8)
        to = pl.multiple_of((band * nb + side * half + o) * share, 8)
        return pltpu.make_async_copy(
            filt.at[o, pl.ds(first, share)], cells.at[pl.ds(to, share)], a2a_l.at[o]
        )

    def stage_c(o):
        wait_halos(f, o, h2_s, h2_r)

        def emit(x, acc):
            start = pl.multiple_of(x * ny, 8)
            filt[o, pl.ds(start, ny), :] = 2.0 * acc - u[o, reach + x, pl.ds(pad, ny), :]

        apply(f, o, emit)
        for j in range(1, group):
            a2a(o, j).start()
        a2a_own(o).start()

    stage_a(0)
    own_pot.wait()
    swap_pot.wait_recv()
    stage_b(0)
    for o in range(1, half):
        stage_a(o)
        stage_c(o - 1)
        stage_b(o)
    stage_c(half - 1)

    for o in range(half):
        a2a_own(o).wait()
        for j in range(1, group):
            a2a(o, j).wait_recv()

    chunk = divisor(share, (16, 8))

    def gather(t):
        return jnp.concatenate(
            [cells[pl.ds(t * chunk + i, total, stride=share), :] for i in range(chunk)], axis=1
        )

    def gram_body(t, acc):
        x = gather(t)
        return acc + lax.dot_general(
            x, x, (((1,), (1,)), ((), ())), precision=HIGHEST, preferred_element_type=jnp.float32
        )

    gram = lax.fori_loop(0, share // chunk, gram_body, jnp.zeros((total, total), jnp.float32))
    gs[...] = jnp.zeros_like(gs)
    gs[0, :, pl.ds(0, total)] = gram
    ar1[me] = gs[0]

    def reduce_1(j):
        return remote(gs.at[0], ar1.at[me], r1_s.at[j - 1], r1_r.at[j - 1], peer_id(j))

    def reduce_2(j):
        return remote(gs.at[1], ar2.at[layer], r2_s.at[j - 1], r2_r.at[j - 1], layer_id(j))

    for j in range(1, group):
        reduce_1(j).start()
    for j in range(1, group):
        reduce_1(j).wait_recv()
    part = ar1[0]
    for j in range(1, group):
        part = part + ar1[j]
    gs[1] = part
    ar2[layer] = part
    for j in range(1, layers):
        reduce_2(j).start()
    for j in range(1, layers):
        reduce_2(j).wait_recv()
    work = ar2[0]
    for j in range(1, layers):
        work = work + ar2[j]

    lane = lax.broadcasted_iota(jnp.int32, work.shape, 1)
    row = lax.broadcasted_iota(jnp.int32, work.shape, 0)
    work = work / jnp.float32(slab * doms * nz)
    work = jnp.where(lane == row + total, jnp.float32(1.0), work)
    for k in range(total):
        root = jnp.sqrt(work[k:k + 1, k:k + 1])
        scale = 1.0 / root
        pivot = work[k:k + 1, :] * scale
        column = work[:, k:k + 1] * scale
        work = jnp.where(row > k, work - column * pivot, jnp.where(row == k, pivot, work))
    inv[...] = work[:, total:2 * total]

    pieces = divisor(share // chunk, (4, 3, 2))
    piece = share // pieces
    obuf3 = obuf.reshape(total, share, nz)

    def ret(s, j):
        b = (band + j) % bands
        at = pl.multiple_of(band * share + s * piece, 8)
        return remote(
            obuf3.at[pl.ds(b * nb, nb), pl.ds(s * piece, piece)],
            out.at[:, pl.ds(at, piece)],
            ret_s.at[j - 1, s], ret_r.at[j - 1, s], {"dom": dom, "band": b},
        )

    def ret_own(s):
        at = pl.multiple_of(band * share + s * piece, 8)
        return pltpu.make_async_copy(
            obuf3.at[pl.ds(band * nb, nb), pl.ds(s * piece, piece)],
            out.at[:, pl.ds(at, piece)], ret_l.at[s],
        )

    for s in range(pieces):
        def ortho_body(t, carry):
            y = jnp.dot(inv[...], gather(t), precision=HIGHEST, preferred_element_type=jnp.float32)
            for i in range(chunk):
                obuf[pl.ds(t * chunk + i, total, stride=share), :] = y[:, i * nz:(i + 1) * nz]
            return carry

        lax.fori_loop(s * (piece // chunk), (s + 1) * (piece // chunk), ortho_body, 0)
        for j in range(1, bands):
            ret(s, j).start()
        ret_own(s).start()

    swap_pot.wait_send()
    for o in range(half):
        swap(o).wait_send()

        @pl.when(has_up)
        def _():
            up(u, o, h1_s, h1_r).wait_send()
            up(f, o, h2_s, h2_r).wait_send()

        @pl.when(has_down)
        def _():
            down(u, o, h1_s, h1_r).wait_send()
            down(f, o, h2_s, h2_r).wait_send()

        for j in range(1, group):
            a2a(o, j).wait_send()
    for j in range(1, group):
        reduce_1(j).wait_send()
    for j in range(1, layers):
        reduce_2(j).wait_send()
    for s in range(pieces):
        ret_own(s).wait()
        for j in range(1, bands):
            ret(s, j).wait()


def shards(doms, bands, orbitals, potential):
    nb, nx, ny, nz = orbitals.shape
    half = nb // 2
    total = nb * bands
    group = 2 * bands
    layers = doms // 2
    slab = nx * ny
    share = slab // bands
    distance = jnp.abs(
        lax.broadcasted_iota(jnp.int32, (nz, nz), 0) - lax.broadcasted_iota(jnp.int32, (nz, nz), 1)
    )
    bz = jnp.zeros((nz, nz), jnp.float32)
    for k in range(1, reach + 1):
        bz = jnp.where(distance == k, jnp.float32(scaled[k]), bz)
    dma = pltpu.SemaphoreType.DMA
    f32 = jnp.float32
    wide = max(nz, 2 * total)
    pieces = divisor(share // divisor(share, (16, 8)), (4, 3, 2))
    out = pl.pallas_call(
        functools.partial(kernel, doms, bands, nb, nx, ny, nz),
        out_shape=jax.ShapeDtypeStruct((nb, slab, nz), f32),
        in_specs=[
            pl.BlockSpec(memory_space=pl.ANY),
            pl.BlockSpec(memory_space=pl.ANY),
            pl.BlockSpec(memory_space=pltpu.VMEM),
        ],
        out_specs=pl.BlockSpec(memory_space=pl.ANY),
        scratch_shapes=[
            pltpu.VMEM((half, 2 * nx + 2 * reach, ny + 2 * pad, nz), f32),
            pltpu.VMEM((half, 2 * nx + 2 * reach, ny + 2 * pad, nz), f32),
            pltpu.VMEM((half, 2 * slab, nz), f32),
            pltpu.VMEM((2 * nx, ny, nz), f32),
            pltpu.VMEM((total * share, nz), f32),
            pltpu.VMEM((total * share, nz), f32),
            pltpu.VMEM((2, total, wide), f32),
            pltpu.VMEM((group, total, wide), f32),
            pltpu.VMEM((layers, total, wide), f32),
            pltpu.VMEM((total, total), f32),
            dma((half,)),
            dma,
            dma((half + 1,)),
            dma((half + 1,)),
            dma((2, half)),
            dma((2, half)),
            dma((2, half)),
            dma((2, half)),
            dma((group - 1, half)),
            dma((group - 1, half)),
            dma((half,)),
            dma((group - 1,)),
            dma((group - 1,)),
            dma((max(layers - 1, 1),)),
            dma((max(layers - 1, 1),)),
            dma((max(bands - 1, 1), pieces)),
            dma((max(bands - 1, 1), pieces)),
            dma((pieces,)),
        ],
        compiler_params=pltpu.CompilerParams(
            collective_id=0, has_side_effects=True, vmem_limit_bytes=56 * 1024 * 1024
        ),
    )(orbitals, potential, bz)
    return out.reshape(orbitals.shape)


def solution(mesh):
    in_specs = (P("band", "dom", None, None), P("dom", None, None))
    out_specs = P("band", "dom", None, None)
    body = functools.partial(shards, mesh.shape["dom"], mesh.shape["band"])
    return jax.shard_map(body, mesh=mesh, in_specs=in_specs, out_specs=out_specs, check_vma=False)
```

time: 323 us -> 140 us (0.43)
  Pallas kernels: 0 us -> 134 us
  waiting for transfers between devices: 132 us -> 0 us
  blocking collectives: 119 us -> 0 us
  other arithmetic: 30.1 us -> 0.67 us
  local copies, waits for them, and re-layouts: 19.7 us -> 3.97 us
  starting transfers between devices: 11 us -> 0 us
  matrix products: 7.36 us -> 0 us
    pallas_call x0 -> x1, Pallas kernels: none -> 134 us  [shards(): pl.pallas_call(functools.partial(kernel, doms, bands, nb, nx, ny, nz), ou...]
    ppermute x4 -> x0, waiting for transfers between devices: 132 us -> none  [the longest x2 101 us: padded_2(): lax.ppermute(lax.slice_in_dim(block, block.shape[dim] - width, None, axis...]
    all_to_all x2 -> x0, blocking collectives: 77.3 us -> none  [the longest x1 39.1 us: shards(): lax.all_to_all(ortho, 'band', split_axis=0, concat_axis=2, tiled=True)]
    psum x1 -> x0, blocking collectives: 41.9 us -> none  [shards(): lax.psum(partial_correlation, ('dom', 'band')) / jnp.float32(all_cells)]
    sub x1 -> x0, other arithmetic: 11.9 us -> none  [shards(): 2.0 * (apply_hamiltonian(padded_first, potential) - center_shift * first)]
    div x3 -> x0, other arithmetic: 11.5 us -> none  [the longest x1 11.5 us: shards(): (apply_hamiltonian(padded, potential) - center_shift * orbitals) / half_w...]
    ppermute x4 -> x0, starting transfers between devices: 11 us -> none  [the longest x2 8.31 us: padded_2(): lax.ppermute(lax.slice_in_dim(block, block.shape[dim] - width, None, axis...]
    dot_general x2 -> x0, matrix products: 7.14 us -> none  [the longest x1 4.57 us: shards(): jnp.dot(inverse, flat, precision=lax.Precision.HIGHEST, preferred_element...]
  transfers between devices with their start and end apart: 4 -> 0, of which waited for: 3 -> 0; matrix products, arithmetic and copies ran while one was open for 0% -> 0% of each run, Pallas kernels for 0% -> 0%
where the time goes in v1:
time: 140 us; the launch traced here: 139 us
  Pallas kernels  134 us (96%)
  local copies, waits for them, and re-layouts  3.97 us (3%)
    pallas_call x1, Pallas kernels, shards(): pl.pallas_call(functools.partial(kernel, doms, bands, nb, nx, ny, nz), ou...  134 us
    unnamed x1, local copies, waits for them, and re-layouts  3.97 us

profile of v1, /device:TPU:5, one launch (start us, length us, event | category | flops | bytes accessed | tf_op | source)
XLA Modules:
  0.0 139.0 jit_solution(11694970176556259428)
XLA Ops:
  0.0 0.7 select_select_fusion.bz
  0.7 134.3 %shard_map.28 = f32[8,768,128]{2,1,0:T(8,128)} custom-call(f32[8,12,64,128]{3,2,1,0:T(8,128)} %orb.1, f32[12,64,128]{2,1,0:T(8,128)} %pot.1, f32[128,128]{1,0:T(8,128)} %select_select_fusion.bz), custom_call_target="tpu_custom_call" | custom-call | tf_op jit(solution)/shard_map/pallas_call | solution.py:364
  135.0 4.0 %copy.4 = f32[8,12,64,128]{3,2,1,0:T(8,128)} copy(f32[8,12,64,128]{3,2,1,0:T(8,128)} %bitcast.1) | data formatting | bytes 6291456

commit v2 on v1

--- a/solution.py
+++ b/solution.py
@@ -30,11 +30,16 @@
     return 1
 
 
+def packed_rows(total, nz):
+    fold = nz // total if total < nz and nz % total == 0 else 1
+    return total // fold if total % (8 * fold) == 0 else total
+
+
 def kernel(
     doms, bands, nb, nx, ny, nz,
-    orb, pot, bz, out,
-    u, f, filt, potb, cells, obuf, gs, ar1, ar2, inv,
-    own_sem, pot_sem, swap_s, swap_r, h1_s, h1_r, h2_s, h2_r,
+    orb, pot, out,
+    bz, u, f, filt, potb, cells, obuf, gs, ar1, ar2, inv,
+    own_sem, pot_sem, pot_s, pot_r, swap_s, swap_r, h1_s, h1_r, h2_s, h2_r,
     a2a_s, a2a_r, a2a_l, r1_s, r1_r, r2_s, r2_r, ret_s, ret_r, ret_l,
 ):
     half = nb // 2
@@ -84,12 +89,23 @@
             orb.at[(1 - side) * half + o], u.at[o, mine, rows], swap_s.at[o], swap_r.at[o], partner
         )
 
-    swap_pot = remote(pot, potb.at[pl.ds(side * nx, nx)], swap_s.at[half], swap_r.at[half], partner)
+    pot_rows = pl.ds(pl.multiple_of(band * share, 8), share)
+    my_pot = pl.ds(pl.multiple_of(side * slab + band * share, 8), share)
+    got_pot = pl.ds(pl.multiple_of((1 - side) * slab + band * share, 8), share)
+    swap_pot = remote(pot.at[pot_rows], potb.at[my_pot], pot_s.at[0], pot_r.at[0], partner)
+
+    def pass_pot(j):
+        return remote(
+            potb.at[got_pot], potb.at[got_pot], pot_s.at[j], pot_r.at[j],
+            {"dom": dom, "band": (band + j) % bands},
+        )
 
     def own(o):
         return pltpu.make_async_copy(orb.at[side * half + o], u.at[o, mine, rows], own_sem.at[o])
 
-    own_pot = pltpu.make_async_copy(pot, potb.at[pl.ds(side * nx, nx)], pot_sem)
+    own_pot = pltpu.make_async_copy(
+        pot, potb.at[pl.ds(pl.multiple_of(side * slab, 8), slab)], pot_sem
+    )
 
     swap(0).start()
     swap_pot.start()
@@ -132,6 +148,13 @@
         def _():
             down(buf, o, s, r).wait_recv()
 
+    distance = jnp.abs(
+        lax.broadcasted_iota(jnp.int32, (nz, nz), 0) - lax.broadcasted_iota(jnp.int32, (nz, nz), 1)
+    )
+    banded = jnp.zeros((nz, nz), jnp.float32)
+    for k in range(1, reach + 1):
+        banded = jnp.where(distance == k, jnp.float32(scaled[k]), banded)
+    bz[...] = banded
     edge = jnp.zeros((planes + 2 * reach, pad, nz), jnp.float32)
     for buf in (u, f):
         for o in range(half):
@@ -160,7 +183,7 @@
             )
             for i in range(step):
                 x = reach + x0 + i
-                weight = potb[x0 + i] * (1.0 / half_width) + (
+                weight = potb[pl.ds(pl.multiple_of((x0 + i) * ny, 8), ny), :] * (1.0 / half_width) + (
                     3.0 * scaled[0] - center_shift / half_width
                 )
                 acc = along_z[i * ny:(i + 1) * ny] + weight * centre[i]
@@ -220,6 +243,10 @@
     stage_a(0)
     own_pot.wait()
     swap_pot.wait_recv()
+    for j in range(1, bands):
+        pass_pot(j).start()
+    for j in range(1, bands):
+        pass_pot(j).wait_recv()
     stage_b(0)
     for o in range(1, half):
         stage_a(o)
@@ -232,6 +259,7 @@
         for j in range(1, group):
             a2a(o, j).wait_recv()
 
+    packed = packed_rows(total, nz)
     chunk = divisor(share, (16, 8))
 
     def gather(t):
@@ -246,9 +274,11 @@
         )
 
     gram = lax.fori_loop(0, share // chunk, gram_body, jnp.zeros((total, total), jnp.float32))
-    gs[...] = jnp.zeros_like(gs)
-    gs[0, :, pl.ds(0, total)] = gram
-    ar1[me] = gs[0]
+    gram = jnp.concatenate(
+        [gram[i * packed:(i + 1) * packed] for i in range(total // packed)], axis=1
+    )
+    gs[0] = gram
+    ar1[me] = gram
 
     def reduce_1(j):
         return remote(gs.at[0], ar1.at[me], r1_s.at[j - 1], r1_r.at[j - 1], peer_id(j))
@@ -273,6 +303,10 @@
     for j in range(1, layers):
         work = work + ar2[j]
 
+    work = jnp.concatenate(
+        [work[:, i * total:(i + 1) * total] for i in range(total // packed)], axis=0
+    )
+    work = jnp.concatenate([work, jnp.zeros((total, total), jnp.float32)], axis=1)
     lane = lax.broadcasted_iota(jnp.int32, work.shape, 1)
     row = lax.broadcasted_iota(jnp.int32, work.shape, 0)
     work = work / jnp.float32(slab * doms * nz)
@@ -318,6 +352,8 @@
         ret_own(s).start()
 
     swap_pot.wait_send()
+    for j in range(1, bands):
+        pass_pot(j).wait_send()
     for o in range(half):
         swap(o).wait_send()
 
@@ -343,6 +379,12 @@
             ret(s, j).wait()
 
 
+def deliver(held, out, sem):
+    copy = pltpu.make_async_copy(held, out, sem)
+    copy.start()
+    copy.wait()
+
+
 def shards(doms, bands, orbitals, potential):
     nb, nx, ny, nz = orbitals.shape
     half = nb // 2
@@ -351,40 +393,37 @@
     layers = doms // 2
     slab = nx * ny
     share = slab // bands
-    distance = jnp.abs(
-        lax.broadcasted_iota(jnp.int32, (nz, nz), 0) - lax.broadcasted_iota(jnp.int32, (nz, nz), 1)
-    )
-    bz = jnp.zeros((nz, nz), jnp.float32)
-    for k in range(1, reach + 1):
-        bz = jnp.where(distance == k, jnp.float32(scaled[k]), bz)
     dma = pltpu.SemaphoreType.DMA
     f32 = jnp.float32
-    wide = max(nz, 2 * total)
+    packed = packed_rows(total, nz)
+    wide = total * total // packed
     pieces = divisor(share // divisor(share, (16, 8)), (4, 3, 2))
     out = pl.pallas_call(
         functools.partial(kernel, doms, bands, nb, nx, ny, nz),
-        out_shape=jax.ShapeDtypeStruct((nb, slab, nz), f32),
+        out_shape=pltpu.VMEM((nb, slab, nz), f32),
         in_specs=[
             pl.BlockSpec(memory_space=pl.ANY),
             pl.BlockSpec(memory_space=pl.ANY),
-            pl.BlockSpec(memory_space=pltpu.VMEM),
         ],
-        out_specs=pl.BlockSpec(memory_space=pl.ANY),
+        out_specs=pl.BlockSpec(memory_space=pltpu.VMEM),
         scratch_shapes=[
+            pltpu.VMEM((nz, nz), f32),
             pltpu.VMEM((half, 2 * nx + 2 * reach, ny + 2 * pad, nz), f32),
             pltpu.VMEM((half, 2 * nx + 2 * reach, ny + 2 * pad, nz), f32),
             pltpu.VMEM((half, 2 * slab, nz), f32),
-            pltpu.VMEM((2 * nx, ny, nz), f32),
+            pltpu.VMEM((2 * slab, nz), f32),
             pltpu.VMEM((total * share, nz), f32),
             pltpu.VMEM((total * share, nz), f32),
-            pltpu.VMEM((2, total, wide), f32),
-            pltpu.VMEM((group, total, wide), f32),
-            pltpu.VMEM((layers, total, wide), f32),
+            pltpu.VMEM((2, packed, wide), f32),
+            pltpu.VMEM((group, packed, wide), f32),
+            pltpu.VMEM((layers, packed, wide), f32),
             pltpu.VMEM((total, total), f32),
             dma((half,)),
             dma,
-            dma((half + 1,)),
-            dma((half + 1,)),
+            dma((bands,)),
+            dma((bands,)),
+            dma((half,)),
+            dma((half,)),
             dma((2, half)),
             dma((2, half)),
             dma((2, half)),
@@ -401,9 +440,16 @@
             dma((pieces,)),
         ],
         compiler_params=pltpu.CompilerParams(
-            collective_id=0, has_side_effects=True, vmem_limit_bytes=56 * 1024 * 1024
+            collective_id=0, has_side_effects=True, vmem_limit_bytes=60 * 1024 * 1024
         ),
-    )(orbitals, potential, bz)
+    )(orbitals, potential.reshape(slab, nz))
+    out = pl.pallas_call(
+        deliver,
+        out_shape=jax.ShapeDtypeStruct((nb, slab, nz), f32),
+        in_specs=[pl.BlockSpec(memory_space=pltpu.VMEM)],
+        out_specs=pl.BlockSpec(memory_space=pl.ANY),
+        scratch_shapes=[dma],
+    )(out)
     return out.reshape(orbitals.shape)
 
 

time: 140 us -> 135 us (0.964)
  local copies, waits for them, and re-layouts: 3.97 us -> 1.65 us
  Pallas kernels: 134 us -> 132 us
    pallas_call x1, Pallas kernels: 134 us -> 129 us  [shards(): pl.pallas_call(functools.partial(kernel, doms, bands, nb, nx, ny, nz), ou...]
    pallas_call x0 -> x1, Pallas kernels: none -> 3.56 us  [shards(): pl.pallas_call(deliver, out_shape=jax.ShapeDtypeStruct((nb, slab, nz), f3...]
    unnamed x1 -> x2, local copies, waits for them, and re-layouts: 3.97 us -> 1.65 us
where the time goes in v2:
time: 135 us; the launch traced here: 134 us
  Pallas kernels  132 us (98%)
  local copies, waits for them, and re-layouts  1.65 us (1%)
    pallas_call x1, Pallas kernels, shards(): pl.pallas_call(functools.partial(kernel, doms, bands, nb, nx, ny, nz), ou...  129 us
    pallas_call x1, Pallas kernels, shards(): pl.pallas_call(deliver, out_shape=jax.ShapeDtypeStruct((nb, slab, nz), f3...  3.56 us

profile of v2, /device:TPU:5, one launch (start us, length us, event | category | flops | bytes accessed | tf_op | source)
XLA Modules:
  0.0 133.9 jit_solution(13412718181910697788)
XLA Ops:
  0.0 128.7 %shard_map.28.held = f32[8,768,128]{2,1,0:T(8,128)S(1)} custom-call(f32[8,12,64,128]{3,2,1,0:T(8,128)} %orb.1, f32[768,128]{1,0:T(8,128)} %bitcast.2), custom_call_target="tpu_custom_call" | custom-call | tf_op jit(solution)/shard_map/pallas_call | solution.py:401
  128.7 0.0 copy-start
  128.7 1.7 %copy-done = f32[8,768,128]{2,1,0:T(8,128)} copy-done((f32[8,768,128]{2,1,0:T(8,128)}, f32[8,768,128]{2,1,0:T(8,128)S(1)}, u32[]{:S(2)}) %copy-start) | copy-done | bytes 3145752
  130.4 3.6 %shard_map.29 = f32[8,768,128]{2,1,0:T(8,128)} custom-call(f32[8,768,128]{2,1,0:T(8,128)} %copy-done), custom_call_target="tpu_custom_call" | custom-call | tf_op jit(solution)/shard_map/pallas_call | solution.py:446
Async XLA Ops:
  128.7 1.7 %copy-start = (f32[8,768,128]{2,1,0:T(8,128)}, f32[8,768,128]{2,1,0:T(8,128)S(1)}, u32[]{:S(2)}) copy-start(f32[8,768,128]{2,1,0:T(8,128)S(1)} %shard_map.28.held) | copy-start | bytes 9437188

commit v3 on v2

--- a/solution.py
+++ b/solution.py
@@ -37,10 +37,11 @@
 
 def kernel(
     doms, bands, nb, nx, ny, nz,
-    orb, pot, out,
-    bz, u, f, filt, potb, cells, obuf, gs, ar1, ar2, inv,
+    orb, pot, full, coef,
+    bz, u, f, filt, potb, cells, gs, ar1, ar2,
     own_sem, pot_sem, pot_s, pot_r, swap_s, swap_r, h1_s, h1_r, h2_s, h2_r,
-    a2a_s, a2a_r, a2a_l, r1_s, r1_r, r2_s, r2_r, ret_s, ret_r, ret_l,
+    out_s, out_r, gram_s, gram_r, gram_l, rest_s, rest_r, pass_s, pass_r, mate_s, mate_r, keep_l,
+    r1_s, r1_r, r2_s, r2_r,
 ):
     half = nb // 2
     planes = 2 * nx
@@ -171,11 +172,11 @@
             def _():
                 buf[o, pl.ds(planes + reach, reach), rows, :] = empty
 
-    step = divisor(planes, (4, 3, 2))
-
-    def apply(buf, o, emit):
+    step = divisor(nx, (4, 3, 2))
+
+    def apply(buf, o, emit, low, count):
         def body(t, carry):
-            x0 = t * step
+            x0 = low + t * step
             centre = [buf[o, reach + x0 + i, pl.ds(pad, ny), :] for i in range(step)]
             along_z = jnp.dot(
                 jnp.concatenate(centre, axis=0), bz[...], precision=HIGHEST,
@@ -196,7 +197,7 @@
                 emit(x0 + i, acc)
             return carry
 
-        lax.fori_loop(0, planes // step, body, 0)
+        lax.fori_loop(0, count // step, body, 0)
 
     def stage_a(o):
         own(o).wait()
@@ -209,36 +210,129 @@
         def emit(x, acc):
             f[o, reach + x, pl.ds(pad, ny), :] = acc
 
-        apply(u, o, emit)
+        apply(u, o, emit, 0, planes)
         send_halos(f, o, h2_s, h2_r)
 
-    def a2a(o, j):
-        q, b = peer(j)
-        first = pl.multiple_of(q * slab + b * share, 8)
-        to = pl.multiple_of((band * nb + side * half + o) * share, 8)
+    towers = bands // 2
+    tower, core = band // 2, band % 2
+    mate = {"dom": dom, "band": tower * 2 + 1 - core}
+
+    def index(k, source):
+        own_side = side if k < half else 1 - side
+        return source * nb + own_side * half + k % half
+
+    def at_full(k, source, first, count):
+        start = pl.multiple_of(index(k, source) * slab + first, 8)
+        return full.at[pl.ds(start, count)]
+
+    def at_cells(k, source):
+        return cells.at[pl.ds(pl.multiple_of(index(k, source) * share, 8), share)]
+
+    def back(o):
         return remote(
-            filt.at[o, pl.ds(first, share)], cells.at[pl.ds(to, share)],
-            a2a_s.at[j - 1, o], a2a_r.at[j - 1, o], peer_id(j),
-        )
-
-    def a2a_own(o):
-        first = pl.multiple_of(me * share, 8)
-        to = pl.multiple_of((band * nb + side * half + o) * share, 8)
+            filt.at[o], at_full(o, band, 0, slab), out_s.at[o], out_r.at[o], partner
+        )
+
+    def spread(k, j):
+        b = (band + j) % bands
+        return remote(
+            at_full(k, band, b * share, share), at_cells(k, band),
+            gram_s.at[j - 1, k], gram_r.at[j - 1, k], {"dom": dom, "band": b},
+        )
+
+    def spread_own(k):
         return pltpu.make_async_copy(
-            filt.at[o, pl.ds(first, share)], cells.at[pl.ds(to, share)], a2a_l.at[o]
-        )
+            at_full(k, band, band * share, share), at_cells(k, band), gram_l.at[k]
+        )
+
+    def lacking(target_tower, target_core):
+        return [((target_tower * 2 + 1 - target_core) * share, share)] + [
+            (((target_tower + a) % towers) * 2 * share, 2 * share) for a in range(1, towers)
+        ]
+
+    def rest(k, jt):
+        return [
+            remote(
+                at_full(k, band, first, count), at_full(k, band, first, count),
+                rest_s.at[jt - 1, k, n], rest_r.at[jt - 1, k, n],
+                {"dom": dom, "band": ((tower + jt) % towers) * 2 + core},
+            )
+            for n, (first, count) in enumerate(lacking((tower + jt) % towers, core))
+        ]
+
+    def to_mate(k):
+        return [
+            remote(
+                at_full(k, band, first, count), at_full(k, band, first, count),
+                mate_s.at[k, n], mate_r.at[k, n], mate,
+            )
+            for n, (first, count) in enumerate(lacking(tower, 1 - core))
+        ]
+
+    def passing(k, jt):
+        source = band - 2 * jt
+        return [
+            remote(
+                at_cells(k, source) if n == 0 else at_full(k, source, first, count),
+                at_full(k, source, first, count),
+                pass_s.at[jt - 1, k, n], pass_r.at[jt - 1, k, n], mate,
+            )
+            for n, (first, count) in enumerate(lacking(tower, 1 - core))
+        ]
+
+    def start_spread(k):
+        for j in range(1, bands):
+            spread(k, j).start()
+        spread_own(k).start()
+
+        @pl.when(core == 0)
+        def _():
+            for copy in to_mate(k):
+                copy.start()
+
+    def start_rest(k):
+        for jt in range(1, towers):
+            @pl.when(tower + jt < towers)
+            def _():
+                for copy in rest(k, jt):
+                    copy.start()
+
+    def start_passing(k):
+        for jt in range(1, towers):
+            spread(k, 2 * jt).wait_recv()
+        start_passing_late(k)
+
+    def start_passing_late(k):
+        for jt in range(1, towers):
+            @pl.when(tower >= jt)
+            def _():
+                for copy in rest(k, jt):
+                    copy.wait_recv()
+                for copy in passing(k, jt):
+                    copy.start()
 
     def stage_c(o):
         wait_halos(f, o, h2_s, h2_r)
 
-        def emit(x, acc):
-            start = pl.multiple_of(x * ny, 8)
-            filt[o, pl.ds(start, ny), :] = 2.0 * acc - u[o, reach + x, pl.ds(pad, ny), :]
-
-        apply(f, o, emit)
-        for j in range(1, group):
-            a2a(o, j).start()
-        a2a_own(o).start()
+        def value(x, acc):
+            return 2.0 * acc - u[o, reach + x, pl.ds(pad, ny), :]
+
+        def emit_other(x, acc):
+            start = pl.multiple_of((x - (1 - side) * nx) * ny, 8)
+            filt[o, pl.ds(start, ny), :] = value(x, acc)
+
+        def emit_own(x, acc):
+            start = pl.multiple_of(index(o, band) * slab + (x - side * nx) * ny, 8)
+            full[pl.ds(start, ny), :] = value(x, acc)
+
+        apply(f, o, emit_other, (1 - side) * nx, nx)
+        back(o).start()
+        apply(f, o, emit_own, side * nx, nx)
+        start_spread(o)
+
+    def stage_x(o):
+        back(o).wait_recv()
+        start_spread(half + o)
 
     stage_a(0)
     own_pot.wait()
@@ -248,16 +342,48 @@
     for j in range(1, bands):
         pass_pot(j).wait_recv()
     stage_b(0)
+    waiting = []
+    passed = []
+    sent = []
+
+    def settle(k):
+        waiting.append(k)
+
+    def issue():
+        if waiting:
+            k = waiting.pop(0)
+            start_rest(k)
+            sent.append(k)
+
     for o in range(1, half):
         stage_a(o)
         stage_c(o - 1)
+        settle(o - 1)
+        if o - 1 < half // 2:
+            issue()
         stage_b(o)
+    if half > 1:
+        stage_x(0)
+        settle(half)
     stage_c(half - 1)
-
-    for o in range(half):
-        a2a_own(o).wait()
-        for j in range(1, group):
-            a2a(o, j).wait_recv()
+    settle(half - 1)
+    issue()
+    for o in range(1 if half > 1 else 0, half):
+        stage_x(o)
+        settle(half + o)
+        if o == half - 2:
+            issue()
+        if o < half - 1 and len(passed) < len(sent):
+            start_passing(sent[len(passed)])
+            passed.append(sent[len(passed)])
+    while waiting:
+        issue()
+
+    for k in range(nb):
+        spread_own(k).wait()
+        for j in range(1, bands):
+            if j % 2 or k not in passed:
+                spread(k, j).wait_recv()
 
     packed = packed_rows(total, nz)
     chunk = divisor(share, (16, 8))
@@ -286,8 +412,24 @@
     def reduce_2(j):
         return remote(gs.at[1], ar2.at[layer], r2_s.at[j - 1], r2_r.at[j - 1], layer_id(j))
 
+    cells3 = cells.reshape(total, share, nz)
+    full3 = full.reshape(total, slab, nz)
+
+    def keep(j):
+        b = (band + j) % bands
+        at = pl.multiple_of(band * share, 8)
+        return pltpu.make_async_copy(
+            cells3.at[pl.ds(b * nb, nb)], full3.at[pl.ds(b * nb, nb), pl.ds(at, share)],
+            keep_l.at[j - 1],
+        )
+
     for j in range(1, group):
         reduce_1(j).start()
+    for j in range(1, bands):
+        keep(j).start()
+    for k in sent[len(passed):half // 2 + 2]:
+        start_passing_late(k)
+        passed.append(k)
     for j in range(1, group):
         reduce_1(j).wait_recv()
     part = ar1[0]
@@ -317,39 +459,39 @@
         pivot = work[k:k + 1, :] * scale
         column = work[:, k:k + 1] * scale
         work = jnp.where(row > k, work - column * pivot, jnp.where(row == k, pivot, work))
-    inv[...] = work[:, total:2 * total]
-
-    pieces = divisor(share // chunk, (4, 3, 2))
-    piece = share // pieces
-    obuf3 = obuf.reshape(total, share, nz)
-
-    def ret(s, j):
-        b = (band + j) % bands
-        at = pl.multiple_of(band * share + s * piece, 8)
-        return remote(
-            obuf3.at[pl.ds(b * nb, nb), pl.ds(s * piece, piece)],
-            out.at[:, pl.ds(at, piece)],
-            ret_s.at[j - 1, s], ret_r.at[j - 1, s], {"dom": dom, "band": b},
-        )
-
-    def ret_own(s):
-        at = pl.multiple_of(band * share + s * piece, 8)
-        return pltpu.make_async_copy(
-            obuf3.at[pl.ds(band * nb, nb), pl.ds(s * piece, piece)],
-            out.at[:, pl.ds(at, piece)], ret_l.at[s],
-        )
-
-    for s in range(pieces):
-        def ortho_body(t, carry):
-            y = jnp.dot(inv[...], gather(t), precision=HIGHEST, preferred_element_type=jnp.float32)
-            for i in range(chunk):
-                obuf[pl.ds(t * chunk + i, total, stride=share), :] = y[:, i * nz:(i + 1) * nz]
-            return carry
-
-        lax.fori_loop(s * (piece // chunk), (s + 1) * (piece // chunk), ortho_body, 0)
-        for j in range(1, bands):
-            ret(s, j).start()
-        ret_own(s).start()
+    solved = jnp.zeros((nb, total), jnp.float32)
+    for b in range(bands):
+        solved = jnp.where(
+            band == b, work[b * nb:(b + 1) * nb, total:2 * total], solved
+        )
+    for n in range(total):
+        for i in range(nb):
+            coef[n, i] = jnp.broadcast_to(solved[i:i + 1, n:n + 1], (8, nz))
+
+    for k in sent:
+        if k not in passed:
+            start_passing_late(k)
+    for k in range(nb):
+        @pl.when(core == 1)
+        def _():
+            for copy in to_mate(k):
+                copy.wait_recv()
+
+        @pl.when(core == 0)
+        def _():
+            for copy in to_mate(k):
+                copy.wait_send()
+
+        for jt in range(1, towers):
+            @pl.when(tower >= jt)
+            def _():
+                for copy in passing(k, jt):
+                    copy.wait()
+
+            @pl.when(tower + jt < towers)
+            def _():
+                for copy in rest(k, jt):
+                    copy.wait_send()
 
     swap_pot.wait_send()
     for j in range(1, bands):
@@ -367,22 +509,58 @@
             down(u, o, h1_s, h1_r).wait_send()
             down(f, o, h2_s, h2_r).wait_send()
 
-        for j in range(1, group):
-            a2a(o, j).wait_send()
+        back(o).wait_send()
+    for k in range(nb):
+        for j in range(1, bands):
+            spread(k, j).wait_send()
     for j in range(1, group):
         reduce_1(j).wait_send()
     for j in range(1, layers):
         reduce_2(j).wait_send()
-    for s in range(pieces):
-        ret_own(s).wait()
-        for j in range(1, bands):
-            ret(s, j).wait()
-
-
-def deliver(held, out, sem):
-    copy = pltpu.make_async_copy(held, out, sem)
-    copy.start()
-    copy.wait()
+    for j in range(1, bands):
+        keep(j).wait()
+
+
+def combine(bands, nb, slab, nz, full, coef, out, held, sem):
+    band = lax.axis_index("band")
+    tile = 8
+    lanes = divisor(slab // tile, (4, 3, 2))
+    blocks = slab // (tile * lanes)
+    parts = divisor(blocks, (4, 3, 2))
+    length = slab // parts
+
+    def copy(part):
+        at = pl.ds(part * length, length)
+        return pltpu.make_async_copy(held.at[:, at], out.at[:, at], sem.at[part])
+
+    def block(t, carry):
+        row = t * (tile * lanes)
+
+        def source(b, acc):
+            acc = list(acc)
+            for n in range(nb):
+                start = pl.multiple_of((b * nb + n) * slab + row, tile)
+                values = [full[pl.ds(start + g * tile, tile), :] for g in range(lanes)]
+                for i in range(nb):
+                    factor = coef[b * nb + n, i]
+                    for g in range(lanes):
+                        acc[i * lanes + g] = acc[i * lanes + g] + factor * values[g]
+            return tuple(acc)
+
+        acc = lax.fori_loop(
+            0, band + 1, source, tuple(jnp.zeros((tile, nz), jnp.float32) for _ in range(nb * lanes))
+        )
+        for i in range(nb):
+            for g in range(lanes):
+                start = pl.multiple_of(row + g * tile, tile)
+                held[i, pl.ds(start, tile), :] = acc[i * lanes + g]
+        return carry
+
+    for part in range(parts):
+        lax.fori_loop(part * (blocks // parts), (part + 1) * (blocks // parts), block, 0)
+        copy(part).start()
+    for part in range(parts):
+        copy(part).wait()
 
 
 def shards(doms, bands, orbitals, potential):
@@ -397,27 +575,29 @@
     f32 = jnp.float32
     packed = packed_rows(total, nz)
     wide = total * total // packed
-    pieces = divisor(share // divisor(share, (16, 8)), (4, 3, 2))
-    out = pl.pallas_call(
+    towers = bands // 2
+    lacks = max(towers, 1)
+    full, coef = pl.pallas_call(
         functools.partial(kernel, doms, bands, nb, nx, ny, nz),
-        out_shape=pltpu.VMEM((nb, slab, nz), f32),
+        out_shape=(pltpu.VMEM((total * slab, nz), f32), pltpu.VMEM((total, nb, 8, nz), f32)),
         in_specs=[
             pl.BlockSpec(memory_space=pl.ANY),
             pl.BlockSpec(memory_space=pl.ANY),
         ],
-        out_specs=pl.BlockSpec(memory_space=pltpu.VMEM),
+        out_specs=(
+            pl.BlockSpec(memory_space=pltpu.VMEM),
+            pl.BlockSpec(memory_space=pltpu.VMEM),
+        ),
         scratch_shapes=[
             pltpu.VMEM((nz, nz), f32),
             pltpu.VMEM((half, 2 * nx + 2 * reach, ny + 2 * pad, nz), f32),
             pltpu.VMEM((half, 2 * nx + 2 * reach, ny + 2 * pad, nz), f32),
-            pltpu.VMEM((half, 2 * slab, nz), f32),
+            pltpu.VMEM((half, slab, nz), f32),
             pltpu.VMEM((2 * slab, nz), f32),
-            pltpu.VMEM((total * share, nz), f32),
             pltpu.VMEM((total * share, nz), f32),
             pltpu.VMEM((2, packed, wide), f32),
             pltpu.VMEM((group, packed, wide), f32),
             pltpu.VMEM((layers, packed, wide), f32),
-            pltpu.VMEM((total, total), f32),
             dma((half,)),
             dma,
             dma((bands,)),
@@ -428,28 +608,39 @@
             dma((2, half)),
             dma((2, half)),
             dma((2, half)),
-            dma((group - 1, half)),
-            dma((group - 1, half)),
             dma((half,)),
+            dma((half,)),
+            dma((bands - 1, nb)),
+            dma((bands - 1, nb)),
+            dma((nb,)),
+            dma((max(towers - 1, 1), nb, lacks)),
+            dma((max(towers - 1, 1), nb, lacks)),
+            dma((max(towers - 1, 1), nb, lacks)),
+            dma((max(towers - 1, 1), nb, lacks)),
+            dma((nb, lacks)),
+            dma((nb, lacks)),
+            dma((bands - 1,)),
             dma((group - 1,)),
             dma((group - 1,)),
             dma((max(layers - 1, 1),)),
             dma((max(layers - 1, 1),)),
-            dma((max(bands - 1, 1), pieces)),
-            dma((max(bands - 1, 1), pieces)),
-            dma((pieces,)),
         ],
         compiler_params=pltpu.CompilerParams(
-            collective_id=0, has_side_effects=True, vmem_limit_bytes=60 * 1024 * 1024
+            collective_id=0, has_side_effects=True, vmem_limit_bytes=48 * 1024 * 1024
         ),
     )(orbitals, potential.reshape(slab, nz))
+    parts = 4
     out = pl.pallas_call(
-        deliver,
+        functools.partial(combine, bands, nb, slab, nz),
         out_shape=jax.ShapeDtypeStruct((nb, slab, nz), f32),
-        in_specs=[pl.BlockSpec(memory_space=pltpu.VMEM)],
+        in_specs=[pl.BlockSpec(memory_space=pltpu.VMEM)] * 2,
         out_specs=pl.BlockSpec(memory_space=pl.ANY),
-        scratch_shapes=[dma],
-    )(out)
+        scratch_shapes=[pltpu.VMEM((nb, slab, nz), f32), dma((parts,))],
+        compiler_params=pltpu.CompilerParams(vmem_limit_bytes=32 * 1024 * 1024),
+    )(
+        pltpu.with_memory_space_constraint(full, pltpu.VMEM),
+        pltpu.with_memory_space_constraint(coef, pltpu.VMEM),
+    )
     return out.reshape(orbitals.shape)
 
 

time: 135 us -> 145 us (1.074)
  Pallas kernels: 132 us -> 145 us
  local copies, waits for them, and re-layouts: 1.65 us -> 0 us
    pallas_call x1, Pallas kernels: 129 us -> 136 us  [shards(): pl.pallas_call(functools.partial(kernel, doms, bands, nb, nx, ny, nz), ou...]
    pallas_call x1, Pallas kernels: 3.56 us -> 8.78 us  [shards(): pl.pallas_call(functools.partial(combine, bands, nb, slab, nz), out_shape...]
    unnamed x2 -> x0, local copies, waits for them, and re-layouts: 1.65 us -> none
where the time goes in v3:
time: 145 us
  Pallas kernels  145 us (100%)
    pallas_call x1, Pallas kernels, shards(): pl.pallas_call(functools.partial(kernel, doms, bands, nb, nx, ny, nz), ou...  136 us
    pallas_call x1, Pallas kernels, shards(): pl.pallas_call(functools.partial(combine, bands, nb, slab, nz), out_shape...  8.78 us

profile of v3, /device:TPU:5, one launch (start us, length us, event | category | flops | bytes accessed | tf_op | source)
XLA Modules:
  0.0 144.9 jit_solution(10009124243465132350)
XLA Ops:
  0.0 136.1 %shard_map.28 = (f32[24576,128]{1,0:T(8,128)S(1)}, f32[32,8,8,128]{3,2,1,0:T(8,128)S(1)}) custom-call(f32[8,12,64,128]{3,2,1,0:T(8,128)} %orb.1, f32[768,128]{1,0:T(8,128)} %bitcast.2), custom_call_target="tpu_custom_call" | custom-call | tf_op jit(solution)/shard_map/pallas_call | solution.py:580
  136.1 8.8 %shard_map.29 = f32[8,768,128]{2,1,0:T(8,128)} custom-call(f32[24576,128]{1,0:T(8,128)S(1)} %get-tuple-element.7.full, f32[32,8,8,128]{3,2,1,0:T(8,128)S(1)} %get-tuple-element.8.coef), custom_call_target="tpu_custom_call" | custom-call | tf_op jit(solution)/shard_map/pallas_call | solution.py:633

commit v4 on v3

--- a/solution.py
+++ b/solution.py
@@ -257,7 +257,7 @@
                 rest_s.at[jt - 1, k, n], rest_r.at[jt - 1, k, n],
                 {"dom": dom, "band": ((tower + jt) % towers) * 2 + core},
             )
-            for n, (first, count) in enumerate(lacking((tower + jt) % towers, core))
+            for n, (first, count) in enumerate(lacking((tower + jt) % towers, core)[1:])
         ]
 
     def to_mate(k):
@@ -270,14 +270,14 @@
         ]
 
     def passing(k, jt):
-        source = band - 2 * jt
+        same, other = band - 2 * jt, (tower - jt) * 2 + 1 - core
+        pieces = [(at_cells(k, same), at_full(k, same, band * share, share))]
+        pieces.append((at_cells(k, other), at_full(k, other, band * share, share)))
+        for first, count in lacking(tower, 1 - core)[1:]:
+            pieces.append((at_full(k, same, first, count), at_full(k, same, first, count)))
         return [
-            remote(
-                at_cells(k, source) if n == 0 else at_full(k, source, first, count),
-                at_full(k, source, first, count),
-                pass_s.at[jt - 1, k, n], pass_r.at[jt - 1, k, n], mate,
-            )
-            for n, (first, count) in enumerate(lacking(tower, 1 - core))
+            remote(src, dst, pass_s.at[jt - 1, k, n], pass_r.at[jt - 1, k, n], mate)
+            for n, (src, dst) in enumerate(pieces)
         ]
 
     def start_spread(k):
@@ -298,8 +298,8 @@
                     copy.start()
 
     def start_passing(k):
-        for jt in range(1, towers):
-            spread(k, 2 * jt).wait_recv()
+        for j in range(1, bands):
+            spread(k, j).wait_recv()
         start_passing_late(k)
 
     def start_passing_late(k):
@@ -382,7 +382,7 @@
     for k in range(nb):
         spread_own(k).wait()
         for j in range(1, bands):
-            if j % 2 or k not in passed:
+            if k not in passed:
                 spread(k, j).wait_recv()
 
     packed = packed_rows(total, nz)
@@ -576,7 +576,7 @@
     packed = packed_rows(total, nz)
     wide = total * total // packed
     towers = bands // 2
-    lacks = max(towers, 1)
+    lacks = towers + 1
     full, coef = pl.pallas_call(
         functools.partial(kernel, doms, bands, nb, nx, ny, nz),
         out_shape=(pltpu.VMEM((total * slab, nz), f32), pltpu.VMEM((total, nb, 8, nz), f32)),

time: 145 us -> 133 us (0.917)
  Pallas kernels: 145 us -> 133 us
    pallas_call x1, Pallas kernels: 136 us -> 124 us  [shards(): pl.pallas_call(functools.partial(kernel, doms, bands, nb, nx, ny, nz), ou...]
where the time goes in v4:
time: 133 us
  Pallas kernels  133 us (100%)
    pallas_call x1, Pallas kernels, shards(): pl.pallas_call(functools.partial(kernel, doms, bands, nb, nx, ny, nz), ou...  124 us
    pallas_call x1, Pallas kernels, shards(): pl.pallas_call(functools.partial(combine, bands, nb, slab, nz), out_shape...  8.78 us

profile of v4, /device:TPU:5, one launch (start us, length us, event | category | flops | bytes accessed | tf_op | source)
XLA Modules:
  0.0 133.2 jit_solution(5834976439249275996)
XLA Ops:
  0.0 124.4 %shard_map.28 = (f32[24576,128]{1,0:T(8,128)S(1)}, f32[32,8,8,128]{3,2,1,0:T(8,128)S(1)}) custom-call(f32[8,12,64,128]{3,2,1,0:T(8,128)} %orb.1, f32[768,128]{1,0:T(8,128)} %bitcast.2), custom_call_target="tpu_custom_call" | custom-call | tf_op jit(solution)/shard_map/pallas_call | solution.py:580
  124.4 8.8 %shard_map.29 = f32[8,768,128]{2,1,0:T(8,128)} custom-call(f32[24576,128]{1,0:T(8,128)S(1)} %get-tuple-element.7.full, f32[32,8,8,128]{3,2,1,0:T(8,128)S(1)} %get-tuple-element.8.coef), custom_call_target="tpu_custom_call" | custom-call | tf_op jit(solution)/shard_map/pallas_call | solution.py:633

commit v5 on v2

--- a/solution.py
+++ b/solution.py
@@ -446,10 +446,11 @@
     out = pl.pallas_call(
         deliver,
         out_shape=jax.ShapeDtypeStruct((nb, slab, nz), f32),
-        in_specs=[pl.BlockSpec(memory_space=pltpu.VMEM)],
+        in_specs=[pl.BlockSpec(memory_space=pl.ANY)],
         out_specs=pl.BlockSpec(memory_space=pl.ANY),
         scratch_shapes=[dma],
-    )(out)
+        compiler_params=pltpu.CompilerParams(vmem_limit_bytes=16 * 1024 * 1024),
+    )(pltpu.with_memory_space_constraint(out, pltpu.VMEM))
     return out.reshape(orbitals.shape)
 
 

time: 135 us -> 132 us (0.978)
  Pallas kernels: 132 us -> 130 us
  local copies, waits for them, and re-layouts: 1.65 us -> 0 us
    pallas_call x1, Pallas kernels: 3.56 us -> 1.67 us  [shards(): pl.pallas_call(deliver, out_shape=jax.ShapeDtypeStruct((nb, slab, nz), f3...]
    unnamed x2 -> x0, local copies, waits for them, and re-layouts: 1.65 us -> none
where the time goes in v5:
time: 132 us; the launch traced here: 130 us
  Pallas kernels  130 us (98%)
    pallas_call x1, Pallas kernels, shards(): pl.pallas_call(functools.partial(kernel, doms, bands, nb, nx, ny, nz), ou...  129 us

profile of v5, /device:TPU:5, one launch (start us, length us, event | category | flops | bytes accessed | tf_op | source)
XLA Modules:
  0.0 130.4 jit_solution(5458285818106617239)
XLA Ops:
  0.0 128.7 %shard_map.28.held = f32[8,768,128]{2,1,0:T(8,128)S(1)} custom-call(f32[8,12,64,128]{3,2,1,0:T(8,128)} %orb.1, f32[768,128]{1,0:T(8,128)} %bitcast.2), custom_call_target="tpu_custom_call" | custom-call | tf_op jit(solution)/shard_map/pallas_call | solution.py:401
  128.7 1.7 %shard_map.29 = f32[8,768,128]{2,1,0:T(8,128)} custom-call(f32[8,768,128]{2,1,0:T(8,128)S(1)} %shard_map.28.held), custom_call_target="tpu_custom_call" | custom-call | tf_op jit(solution)/shard_map/pallas_call | solution.py:446

commit v6 on v5

--- a/solution.py
+++ b/solution.py
@@ -319,7 +319,7 @@
         work = jnp.where(row > k, work - column * pivot, jnp.where(row == k, pivot, work))
     inv[...] = work[:, total:2 * total]
 
-    pieces = divisor(share // chunk, (4, 3, 2))
+    pieces = divisor(share // chunk, (6, 4, 3, 2))
     piece = share // pieces
     obuf3 = obuf.reshape(total, share, nz)
 
@@ -397,7 +397,7 @@
     f32 = jnp.float32
     packed = packed_rows(total, nz)
     wide = total * total // packed
-    pieces = divisor(share // divisor(share, (16, 8)), (4, 3, 2))
+    pieces = divisor(share // divisor(share, (16, 8)), (6, 4, 3, 2))
     out = pl.pallas_call(
         functools.partial(kernel, doms, bands, nb, nx, ny, nz),
         out_shape=pltpu.VMEM((nb, slab, nz), f32),

time: 132 us -> 132 us (level)
  no operation moved by 1% of the time
where the time goes in v6:
time: 132 us; the launch traced here: 130 us
  Pallas kernels  130 us (98%)
    pallas_call x1, Pallas kernels, shards(): pl.pallas_call(functools.partial(kernel, doms, bands, nb, nx, ny, nz), ou...  128 us

profile of v6, /device:TPU:5, one launch (start us, length us, event | category | flops | bytes accessed | tf_op | source)
XLA Modules:
  0.0 130.1 jit_solution(7256682265786835484)
XLA Ops:
  0.0 128.4 %shard_map.28.held = f32[8,768,128]{2,1,0:T(8,128)S(1)} custom-call(f32[8,12,64,128]{3,2,1,0:T(8,128)} %orb.1, f32[768,128]{1,0:T(8,128)} %bitcast.2), custom_call_target="tpu_custom_call" | custom-call | tf_op jit(solution)/shard_map/pallas_call | solution.py:401
  128.4 1.7 %shard_map.29 = f32[8,768,128]{2,1,0:T(8,128)} custom-call(f32[8,768,128]{2,1,0:T(8,128)S(1)} %shard_map.28.held), custom_call_target="tpu_custom_call" | custom-call | tf_op jit(solution)/shard_map/pallas_call | solution.py:446
